TPU v7x, 256 devices: a whole 4x4x8 slice. The times are simulated.
256 devices in a mesh: group: 16 (over y, x), member: 16 (over z, core).
Axes of the slice: x: 4, y: 4, z: 8, core: 2. Of those that a mesh axis runs over, the one named last changes fastest.
Arguments:
- queries: bfloat16 [65536, 6144], P(('group', 'member')), may hold values from -64 to 64
- keys_values: bfloat16 [512, 128, 2048], P('group', 'member'), may hold values from -8 to 8
- local_lists: int32 [512, 5], P(('group', 'member')), may hold values from -1 to 31, as said below
- remote_lists: int32 [512, 3], P(('group', 'member')), may hold values from -1 to 15, as said below
- send_blocks: int32 [16, 16], P('group'), may hold values from 0 to 31
Outputs:
- attended: bfloat16 [65536, 6144], P(('group', 'member'))
Inputs may be any that keep to these rules, and one draw needn't show every extreme that they name: `local_lists`: row i lists distinct blocks of its slab, numbered 0 to 31 within the slab, then -1 in the remaining entries; the first entry is i mod 32, the row's own block. Some row lists 5 blocks. `remote_lists`: row i lists distinct slabs other than its own slab i // 32, then -1 in the remaining entries; a row may list none. Some row lists 3 slabs.
All inputs are finite; a program needn't handle non-finite values.
Results may differ from a plain program's by a relative error of at most 0.0038.
Values may be sent and summed in bfloat16 or wider, within the bound.
A program may use at most 128 MiB of HBM per device.

v0:
```python
import jax
import jax.numpy as jnp
from jax import lax
from jax.sharding import PartitionSpec as P

HEADS = 48
KV_HEADS = 8
HEAD_DIM = 128


def attend_rows(query_rows, listed, usable):
    block_rows = query_rows.shape[0]
    key_width = KV_HEADS * HEAD_DIM
    repeat = HEADS // KV_HEADS
    query_heads = query_rows.reshape(block_rows, KV_HEADS, repeat, HEAD_DIM)
    keys_all = listed[:, :, :key_width].reshape(
        listed.shape[0], listed.shape[1], KV_HEADS, HEAD_DIM
    )
    values_all = listed[:, :, key_width:].reshape(
        listed.shape[0], listed.shape[1], KV_HEADS, HEAD_DIM
    )
    halves = 2
    head_span = KV_HEADS // halves
    pieces = []
    for part_index in range(halves):
        start_head = part_index * head_span
        query_part = query_heads[:, start_head : start_head + head_span]
        keys_part = keys_all[:, :, start_head : start_head + head_span]
        values_part = values_all[:, :, start_head : start_head + head_span]
        scores = jnp.einsum(
            "qgrd,pkgd->qgrpk", query_part, keys_part, preferred_element_type=jnp.float32
        )
        scores = scores * HEAD_DIM ** (-0.5)
        scores = jnp.where(usable[:, None], scores, -jnp.inf)
        maxima = jnp.max(scores, axis=(3, 4), keepdims=True)
        weights = jnp.exp(scores - maxima)
        totals = jnp.sum(weights, axis=(3, 4))
        rounded = weights.astype(jnp.bfloat16)
        blended = jnp.einsum(
            "qgrpk,pkgd->qgrd", rounded, values_part, preferred_element_type=jnp.float32
        )
        pieces.append(blended / totals[..., None])
    joined = jnp.concatenate(pieces, axis=1)
    return joined.reshape(block_rows, HEADS * HEAD_DIM).astype(jnp.bfloat16)


def shards(queries, keys_values, local_lists, remote_lists, send_blocks):
    targets = send_blocks[0]
    query_count = local_lists.shape[0]
    block_rows = queries.shape[0] // query_count
    outputs = []
    outgoing = jnp.take(keys_values, targets, axis=0)
    arrived = lax.all_to_all(outgoing, "group", split_axis=0, concat_axis=0, tiled=True)
    group_pool = lax.all_gather(keys_values, "member", axis=1, tiled=True)
    cast_pool = lax.all_gather(arrived, "member", axis=1, tiled=True)
    for query_block in range(query_count):
        local_row = local_lists[query_block]
        remote_row = remote_lists[query_block]
        listed = jnp.concatenate(
            [
                jnp.take(group_pool, jnp.maximum(local_row, 0), axis=0),
                jnp.take(cast_pool, jnp.maximum(remote_row, 0), axis=0),
            ],
            axis=0,
        )
        usable = jnp.concatenate([local_row >= 0, remote_row >= 0])
        query_rows = queries[query_block * block_rows : (query_block + 1) * block_rows]
        outputs.append(attend_rows(query_rows, listed, usable))
    return jnp.concatenate(outputs, axis=0)


def solution(mesh):
    placed = (
        P(("group", "member"), None),
        P("group", "member", None),
        P(("group", "member"), None),
        P(("group", "member"), None),
        P("group", None),
    )
    return jax.shard_map(
        shards, mesh=mesh, in_specs=placed, out_specs=P(("group", "member"), None), check_vma=False
    )
```

profile of v0, /device:TPU:1, one launch (start us, length us, event | category | flops | bytes accessed | tf_op | source)
XLA Modules:
  0.0 306.8 jit_solution(815406715089342255)
XLA Ops:
  6.5 0.7 fusion.54
  7.2 0.7 compare_and_fusion.4
  7.9 1.8 gather_fusion
  9.7 0.1 broadcast_select_fusion.4
  9.8 17.9 %all_to_all.5 = bf16[16,8,2048]{2,1,0:T(8,128)(2,1)} all-to-all(bf16[16,8,2048]{2,1,0:T(8,128)(2,1)S(1)} %broadcast_select_fusion.4), channel_id=1, replica_groups=mesh['group'=16,'member'=16] {'group'}, dimensions={0} | all-to-all | bytes 1048576 | tf_op jit(solution)/shard_map/all_to_all | solution.py:53
  27.7 0.0 all-gather.3.cloned.1.call-start
  27.8 0.7 all-gather.3.cloned.1.call-update
  28.5 2.1 fusion.63
  30.6 1.6 copy.82
  32.2 1.6 copy.89
  33.8 0.1 pad_add_fusion
  34.0 50.6 %all-gather.5.cloned.1.call-done = bf16[16,128,2048]{2,1,0:T(8,128)(2,1)} async-done(((bf16[16,8,2048]{2,1,0:T(8,128)(2,1)}), bf16[16,128,2048]{2,1,0:T(8,128)(2,1)}) %all-gather.5.cloned.1.call-update) | async-done | bytes 8388624 | tf_op jit(solution)/shard_map/all_gather | solution.py:55
  84.6 4.0 %gather_fusion.4 = bf16[3,128,2048]{2,1,0:T(8,128)(2,1)S(1)} fusion(bf16[16,128,2048]{2,1,0:T(8,128)(2,1)} %all-gather.5.cloned.1.call-done, s32[1024]{0:T(1024)S(1)} %pad_clamp_fusion), kind=kCustom, calls=%fused_computation.3.clone | custom fusion | bytes 3145740 | tf_op jit(solution)/shard_map/jit(_take)/gather | solution.py:62
  88.6 4.0 %gather_fusion.2 = bf16[3,128,2048]{2,1,0:T(8,128)(2,1)S(1)} fusion(bf16[16,128,2048]{2,1,0:T(8,128)(2,1)} %all-gather.5.cloned.1.call-done, s32[1024]{0:T(1024)S(1)} %pad_clamp_fusion.2), kind=kCustom, calls=%fused_computation.1.clone | custom fusion | bytes 3145740 | tf_op jit(solution)/shard_map/jit(_take)/gather | solution.py:62
  92.7 2.0 broadcast_select_fusion.2
  94.7 85.7 %all-gather.3.cloned.1.call-done = bf16[32,128,2048]{2,1,0:T(8,128)(2,1)} async-done(((bf16[32,8,2048]{2,1,0:T(8,128)(2,1)}), bf16[32,128,2048]{2,1,0:T(8,128)(2,1)}) %all-gather.3.cloned.1.call-update) | async-done | bytes 16777232 | tf_op jit(solution)/shard_map/all_gather | solution.py:54
  180.4 8.1 %gather_fusion.3 = bf16[5,128,2048]{2,1,0:T(8,128)(2,1)} fusion(bf16[32,128,2048]{2,1,0:T(8,128)(2,1)} %all-gather.3.cloned.1.call-done, s32[1024]{0:T(1024)S(1)} %pad_clamp_fusion.1), kind=kCustom, calls=%fused_computation.2.clone | custom fusion | bytes 5242900 | tf_op jit(solution)/shard_map/jit(_take)/gather | solution.py:61
  188.5 8.1 %gather_fusion.1 = bf16[5,128,2048]{2,1,0:T(8,128)(2,1)} fusion(bf16[32,128,2048]{2,1,0:T(8,128)(2,1)} %all-gather.3.cloned.1.call-done, s32[1024]{0:T(1024)S(1)} %pad_clamp_fusion.4), kind=kCustom, calls=%fused_computation.clone | custom fusion | bytes 5242900 | tf_op jit(solution)/shard_map/jit(_take)/gather | solution.py:61
  196.7 3.2 %broadcast_select_fusion = (bf16[5,128,2048]{2,1,0:T(8,128)(2,1)S(1)}, bf16[5,128,2048]{2,1,0:T(8,128)(2,1)S(1)}) fusion(bf16[5,128,2048]{2,1,0:T(8,128)(2,1)} %gather_fusion.3, pred[5]{0:T(512)(128)(4,1)S(1)} %get-tuple-element.37, bf16[5,128,2048]{2,1,0:T(8,128)(2,1)} %gather_fusion.1, pred[5]{0:T(512)(128)(4,1)S(1)} %get-tuple-element.11), kind=kLoop, calls=%fused_computation.42 | loop fusion | flops 2621440 | bytes 10485770 | tf_op jit(solution)/shard_map/jit(_take)/select_n | solution.py:61
  199.9 2.3 fusion.24
  202.1 3.9 %copy.43 = bf16[8,128,1024]{1,2,0:T(8,128)(2,1)} copy(bf16[8,128,1024]{2,1,0:T(8,128)(2,1)} %get-tuple-element.21) | data formatting | bytes 4194304 | tf_op jit(solution)/shard_map/slice | solution.py:19
  206.0 3.1 %fusion.66 = (bf16[8,128,4,128]{1,3,2,0:T(8,128)(2,1)}, bf16[8,128,4,128]{1,3,2,0:T(8,128)(2,1)}) fusion(bf16[8,128,8,128]{1,3,2,0:T(8,128)(2,1)} %bitcast.206), kind=kLoop, calls=%fused_computation.115 | loop fusion | bytes 4194304 | tf_op jit(solution)/shard_map/slice | solution.py:29
  209.1 3.9 %copy.45 = bf16[8,128,1024]{1,2,0:T(8,128)(2,1)} copy(bf16[8,128,1024]{2,1,0:T(8,128)(2,1)} %get-tuple-element.22) | data formatting | bytes 4194304 | tf_op jit(solution)/shard_map/slice | solution.py:16
  213.0 3.1 %fusion.67 = (bf16[8,128,4,128]{1,3,2,0:T(8,128)(2,1)}, bf16[8,128,4,128]{1,3,2,0:T(8,128)(2,1)}) fusion(bf16[8,128,8,128]{1,3,2,0:T(8,128)(2,1)} %bitcast.207), kind=kLoop, calls=%fused_computation.116 | loop fusion | bytes 4194304 | tf_op jit(solution)/shard_map/slice | solution.py:28
  216.2 2.3 copy.88
  218.4 2.3 copy.92
  220.7 3.4 %fusion.25 = (bf16[8,128,1024]{2,1,0:T(8,128)(2,1)}, bf16[8,128,1024]{2,1,0:T(8,128)(2,1)}) fusion(bf16[5,128,2048]{2,1,0:T(8,128)(2,1)S(1)} %get-tuple-element.48, bf16[3,128,2048]{2,1,0:T(8,128)(2,1)} %get-tuple-element.50), kind=kLoop, calls=%fused_computation.45 | loop fusion | flops 8388608 | bytes 8388608 | tf_op jit(solution)/shard_map/concatenate | solution.py:59
  224.2 3.0 copy.32
  227.2 1.5 fusion.64
  228.7 3.0 copy.34
  231.7 1.5 fusion.65
  233.2 2.4 copy.81
  235.6 2.3 copy.85
  237.9 6.3 %bitcast_reduce_fusion.1 = (f32[128,4,6]{0,2,1:T(8,128)S(1)}, f32[4,8,128,128,6]{3,2,4,1,0:T(8,128)}) fusion(pred[8]{0:T(512)(128)(4,1)S(1)} %get-tuple-element.52, bf16[128,8,6,128]{0,3,2,1:T(8,128)(2,1)S(1)} %bitcast.214, bf16[8,128,4,128]{3,1,0,2:T(8,128)(2,1)S(1)} %copy-done.1), kind=kOutput, calls=%fused_computation.9 | convolution fusion | flops 814740480 | bytes 14430720 | tf_op jit(solution)/shard_map/qgrd,pkgd->qgrpk/dot_general | solution.py:30
  244.2 7.5 %fusion.8 = (f32[128,4,6]{0,2,1:T(8,128)S(1)}, f32[128,4,6]{0,2,1:T(8,128)S(1)}, f32[4,8,128,128,6]{3,2,4,1,0:T(8,128)S(1)}) fusion(f32[4,8,128,128,6]{3,2,4,1,0:T(8,128)} %get-tuple-element.42, f32[128,4,6]{0,2,1:T(8,128)S(1)} %get-tuple-element.41, pred[8]{0:T(512)(128)(4,1)S(1)} %get-tuple-element.52, bf16[128,8,6,128]{0,3,2,1:T(8,128)(2,1)S(1)} %bitcast.215, ...), kind=kOutput, calls=%fused_computation.25 | convolution fusion | flops 827320320 | bytes 27042304 | tf_op jit(solution)/shard_map/qgrd,pkgd->qgrpk/dot_general | solution.py:30
  251.7 7.6 %fusion.27 = bf16[128,4,6,128]{0,3,2,1:T(8,128)(2,1)S(1)} fusion(f32[4,8,128,128,6]{3,2,4,1,0:T(8,128)} %get-tuple-element.42, f32[128,4,6]{0,2,1:T(8,128)S(1)} %get-tuple-element.41, pred[8]{0:T(512)(128)(4,1)S(1)} %get-tuple-element.52, bf16[8,128,4,128]{1,3,2,0:T(8,128)(2,1)S(1)} %copy-done.9, f32[128,4,6]{0,2,1:T(8,128)S(1)} %get-tuple-element.9), kind=kOutput, calls=%fused_computation.51 | convolution fusion | flops 818675712 | bytes 14442504 | tf_op jit(solution)/shard_map/qgrpk,pkgd->qgrd/dot_general | solution.py:39
  259.3 2.5 fusion.10
  261.9 3.3 %fusion.26 = bf16[128,4,6,128]{0,3,2,1:T(8,128)(2,1)S(1)} fusion(f32[4,8,128,128,6]{3,2,4,1,0:T(8,128)S(1)} %get-tuple-element.43, f32[128,4,6]{0,2,1:T(8,128)S(1)} %get-tuple-element.10, pred[8]{0:T(512)(128)(4,1)S(1)} %get-tuple-element.52, bf16[8,128,4,128]{1,3,2,0:T(8,128)(2,1)S(1)} %copy-done.7, f32[128,4,6]{0,2,1:T(8,128)S(1)} %fusion.10), kind=kOutput, calls=%fused_computation.49 | convolution fusion | flops 818675712 | bytes 14442504 | tf_op jit(solution)/shard_map/qgrpk,pkgd->qgrd/dot_general | solution.py:39
  265.1 0.1 pad_maximum_fusion.4
  265.3 0.7 copy.55
  266.0 7.9 %bitcast_reduce_fusion.3 = (f32[128,4,6]{0,2,1:T(8,128)S(1)}, f32[4,8,128,128,6]{3,2,4,1,0:T(8,128)}) fusion(pred[8]{0:T(512)(128)(4,1)S(1)} %get-tuple-element.51, bf16[128,8,6,128]{0,3,2,1:T(8,128)(2,1)} %bitcast.212, bf16[8,128,4,128]{3,1,0,2:T(8,128)(2,1)} %copy.81), kind=kOutput, calls=%fused_computation.15 | convolution fusion | flops 814740480 | bytes 14430216 | tf_op jit(solution)/shard_map/qgrd,pkgd->qgrpk/dot_general | solution.py:30
  273.9 7.5 %fusion.4 = (f32[128,4,6]{0,2,1:T(8,128)S(1)}, f32[128,4,6]{0,2,1:T(8,128)S(1)}, f32[4,8,128,128,6]{3,2,4,1,0:T(8,128)S(1)}) fusion(f32[4,8,128,128,6]{3,2,4,1,0:T(8,128)} %get-tuple-element.45, f32[128,4,6]{0,2,1:T(8,128)S(1)} %get-tuple-element.44, pred[8]{0:T(512)(128)(4,1)S(1)} %get-tuple-element.51, bf16[128,8,6,128]{0,3,2,1:T(8,128)(2,1)S(1)} %bitcast.213, ...), kind=kOutput, calls=%fused_computation.21 | convolution fusion | flops 827320320 | bytes 27042304 | tf_op jit(solution)/shard_map/qgrd,pkgd->qgrpk/dot_general | solution.py:30
  281.4 7.6 %fusion.29 = bf16[128,4,6,128]{0,3,2,1:T(8,128)(2,1)S(1)} fusion(f32[4,8,128,128,6]{3,2,4,1,0:T(8,128)} %get-tuple-element.45, f32[128,4,6]{0,2,1:T(8,128)S(1)} %get-tuple-element.44, pred[8]{0:T(512)(128)(4,1)S(1)} %get-tuple-element.51, bf16[8,128,4,128]{1,3,2,0:T(8,128)(2,1)S(1)} %copy-done.8, f32[128,4,6]{0,2,1:T(8,128)S(1)} %get-tuple-element.6), kind=kOutput, calls=%fused_computation.55 | convolution fusion | flops 818675712 | bytes 14442504 | tf_op jit(solution)/shard_map/qgrpk,pkgd->qgrd/dot_general | solution.py:39
  289.1 2.5 fusion.6
  291.6 3.3 %fusion.28 = bf16[128,4,6,128]{0,3,2,1:T(8,128)(2,1)S(1)} fusion(f32[4,8,128,128,6]{3,2,4,1,0:T(8,128)S(1)} %get-tuple-element.46, f32[128,4,6]{0,2,1:T(8,128)S(1)} %get-tuple-element.8, pred[8]{0:T(512)(128)(4,1)S(1)} %get-tuple-element.51, bf16[8,128,4,128]{1,3,2,0:T(8,128)(2,1)S(1)} %copy-done.6, f32[128,4,6]{0,2,1:T(8,128)S(1)} %fusion.6), kind=kOutput, calls=%fused_computation.53 | convolution fusion | flops 818675712 | bytes 14442504 | tf_op jit(solution)/shard_map/qgrpk,pkgd->qgrd/dot_general | solution.py:39
  294.9 0.1 pad_maximum_fusion.3
  295.0 1.6 copy.54
  296.6 3.3 %pad_maximum_fusion = bf16[256,6144]{1,0:T(8,128)(2,1)} fusion(bf16[128,6144]{1,0:T(8,128)(2,1)S(1)} %copy.55, bf16[128,6144]{1,0:T(8,128)(2,1)} %copy.54), kind=kLoop, calls=%fused_computation.41 | loop fusion | flops 6291456 | bytes 6291456 | tf_op jit(solution)/shard_map/concatenate | solution.py:69
  (35 shorter events, 0.1 us)
Async XLA Ops:
  6.5 78.1 %all-gather.5.cloned.1.call-start = ((), (), s32[]{:S(2)}) async-start(), calls=%async_computation.2 | async-start | bytes 8912896 | tf_op jit(solution)/shard_map/all_gather | solution.py:55
  27.7 152.7 %all-gather.3.cloned.1.call-start = ((), (), s32[]{:S(2)}) async-start(), calls=%async_computation.1 | async-start | bytes 17825792 | tf_op jit(solution)/shard_map/all_gather | solution.py:54
  30.6 3.2 %copy-start.11 = (s32[2,5]{1,0:T(2,128)S(1)}, s32[2,5]{1,0:T(2,128)}, u32[]{:S(2)}) copy-start(s32[2,5]{1,0:T(2,128)} %param.11) | copy-start | bytes 124
  30.6 3.2 %copy-start.10 = (s32[2,3]{1,0:T(2,128)S(1)}, s32[2,3]{1,0:T(2,128)}, u32[]{:S(2)}) copy-start(s32[2,3]{1,0:T(2,128)} %param.12) | copy-start | bytes 76
  196.7 3.2 %copy-start = (bf16[3,128,2048]{2,1,0:T(8,128)(2,1)S(1)}, bf16[3,128,2048]{2,1,0:T(8,128)(2,1)}, u32[]{:S(2)}) copy-start(bf16[3,128,2048]{2,1,0:T(8,128)(2,1)} %get-tuple-element.49) | copy-start | bytes 4718596
  231.7 6.2 %copy-start.1 = (bf16[8,128,4,128]{3,1,0,2:T(8,128)(2,1)S(1)}, bf16[8,128,4,128]{3,1,0,2:T(8,128)(2,1)}, u32[]{:S(2)}) copy-start(bf16[8,128,4,128]{3,1,0,2:T(8,128)(2,1)} %copy.88) | copy-start | bytes 3145732
  233.2 4.7 %copy-start.3 = (bf16[128,6144]{0,1:T(8,128)(2,1)S(1)}, bf16[128,6144]{0,1:T(8,128)(2,1)}, u32[]{:S(2)}) copy-start(bf16[128,6144]{0,1:T(8,128)(2,1)} %copy.89) | copy-start | bytes 4718596
  237.9 6.3 %copy-start.5 = (bf16[8,128,4,128]{3,1,0,2:T(8,128)(2,1)S(1)}, bf16[8,128,4,128]{3,1,0,2:T(8,128)(2,1)}, u32[]{:S(2)}) copy-start(bf16[8,128,4,128]{3,1,0,2:T(8,128)(2,1)} %copy.92) | copy-start | bytes 3145732
  244.2 7.5 %copy-start.9 = (bf16[8,128,4,128]{1,3,2,0:T(8,128)(2,1)S(1)}, bf16[8,128,4,128]{1,3,2,0:T(8,128)(2,1)}, u32[]{:S(2)}) copy-start(bf16[8,128,4,128]{1,3,2,0:T(8,128)(2,1)} %get-tuple-element.29) | copy-start | bytes 3145732
  259.3 2.5 copy-start.7
  266.0 7.9 %copy-start.2 = (bf16[128,6144]{0,1:T(8,128)(2,1)S(1)}, bf16[128,6144]{0,1:T(8,128)(2,1)}, u32[]{:S(2)}) copy-start(bf16[128,6144]{0,1:T(8,128)(2,1)} %copy.82) | copy-start | bytes 4718596
  266.0 7.9 %copy-start.4 = (bf16[8,128,4,128]{3,1,0,2:T(8,128)(2,1)S(1)}, bf16[8,128,4,128]{3,1,0,2:T(8,128)(2,1)}, u32[]{:S(2)}) copy-start(bf16[8,128,4,128]{3,1,0,2:T(8,128)(2,1)} %copy.85) | copy-start | bytes 3145732
  273.9 7.5 %copy-start.8 = (bf16[8,128,4,128]{1,3,2,0:T(8,128)(2,1)S(1)}, bf16[8,128,4,128]{1,3,2,0:T(8,128)(2,1)}, u32[]{:S(2)}) copy-start(bf16[8,128,4,128]{1,3,2,0:T(8,128)(2,1)} %get-tuple-element.25) | copy-start | bytes 3145732
  289.1 2.5 copy-start.6
Sparse Core Ops, SparseCore 0:
  27.8 56.7 all-gather.4
  86.5 93.9 all-gather.2
where the time goes:
time: 308 us; the launch traced here: 307 us
  waiting for transfers between devices  137 us (44%)
  local copies, waits for them, and re-layouts  66 us (21%)
  matrix products  51 us (17%)
  other arithmetic  21.1 us (7%)
  blocking collectives  17.9 us (6%)
  between operations  13.7 us (4%)
    all_gather x1, waiting for transfers between devices, shards(): group_pool = lax.all_gather(keys_values, 'member', axis=1, tiled=True)  85.7 us
    all_gather x1, waiting for transfers between devices, shards(): cast_pool = lax.all_gather(arrived, 'member', axis=1, tiled=True)  50.6 us
    dot_general x4, matrix products, attend_rows(): jnp.einsum('qgrd,pkgd->qgrpk', query_part, keys_part, preferred_element_t...  29.2 us
    dot_general x4, matrix products, attend_rows(): jnp.einsum('qgrpk,pkgd->qgrd', rounded, values_part, preferred_element_ty...  21.8 us
    all_to_all x1, blocking collectives, shards(): lax.all_to_all(outgoing, 'group', split_axis=0, concat_axis=0, tiled=True)  17.9 us
    gather x2, local copies, waits for them, and re-layouts, shards(): jnp.take(group_pool, jnp.maximum(local_row, 0), axis=0)  16.3 us
    unnamed x30, local copies, waits for them, and re-layouts  12.5 us
    gather x2, local copies, waits for them, and re-layouts, shards(): jnp.take(cast_pool, jnp.maximum(remote_row, 0), axis=0)  8.06 us
  transfers between devices with their start and end apart: 2, of which 2 were waited for; matrix products, arithmetic and copies ran while one was open for 5% of the time, Pallas kernels for 0%

commit v1 on v0

--- a/solution.py
+++ b/solution.py
@@ -51,8 +51,13 @@
     outputs = []
     outgoing = jnp.take(keys_values, targets, axis=0)
     arrived = lax.all_to_all(outgoing, "group", split_axis=0, concat_axis=0, tiled=True)
-    group_pool = lax.all_gather(keys_values, "member", axis=1, tiled=True)
-    cast_pool = lax.all_gather(arrived, "member", axis=1, tiled=True)
+    group_pool, cast_pool = jnp.split(
+        lax.all_gather(
+            jnp.concatenate([keys_values, arrived], axis=0), "member", axis=1, tiled=True
+        ),
+        [keys_values.shape[0]],
+        axis=0,
+    )
     for query_block in range(query_count):
         local_row = local_lists[query_block]
         remote_row = remote_lists[query_block]

time: 308 us -> 328 us (1.065)
  local copies, waits for them, and re-layouts: 66 us -> 92.2 us
  waiting for transfers between devices: 137 us -> 130 us
    split x0 -> x2, local copies, waits for them, and re-layouts: none -> 22.4 us  [shards(): jnp.split(lax.all_gather(jnp.concatenate([keys_values, arrived], axis=0),...]
    all_gather x2 -> x1, waiting for transfers between devices: 136 us -> 130 us  [shards(): lax.all_gather(jnp.concatenate([keys_values, arrived], axis=0), 'member',...]
  transfers between devices with their start and end apart: 2 -> 1, of which waited for: 2 -> 1; matrix products, arithmetic and copies ran while one was open for 5% -> 2% of each run, Pallas kernels for 0% -> 0%
where the time goes in v1:
time: 328 us; the launch traced here: 327 us
  waiting for transfers between devices  130 us (40%)
  local copies, waits for them, and re-layouts  92.2 us (28%)
  matrix products  48.9 us (15%)
  other arithmetic  24.3 us (7%)
  blocking collectives  17.8 us (5%)
  between operations  13.7 us (4%)
    all_gather x1, waiting for transfers between devices, shards(): lax.all_gather(jnp.concatenate([keys_values, arrived], axis=0), 'member',...  130 us
    dot_general x4, matrix products, attend_rows(): jnp.einsum('qgrd,pkgd->qgrpk', query_part, keys_part, preferred_element_t...  27.2 us
    split x2, local copies, waits for them, and re-layouts, shards(): jnp.split(lax.all_gather(jnp.concatenate([keys_values, arrived], axis=0),...  22.4 us
    dot_general x4, matrix products, attend_rows(): jnp.einsum('qgrpk,pkgd->qgrd', rounded, values_part, preferred_element_ty...  21.7 us
    all_to_all x1, blocking collectives, shards(): lax.all_to_all(outgoing, 'group', split_axis=0, concat_axis=0, tiled=True)  17.8 us
    gather x2, local copies, waits for them, and re-layouts, shards(): jnp.take(group_pool, jnp.maximum(local_row, 0), axis=0)  16.3 us
    unnamed x30, local copies, waits for them, and re-layouts  12.6 us
    gather x2, local copies, waits for them, and re-layouts, shards(): jnp.take(cast_pool, jnp.maximum(remote_row, 0), axis=0)  10.4 us
  transfers between devices with their start and end apart: 1, of which 1 were waited for; matrix products, arithmetic and copies ran while one was open for 2% of the time, Pallas kernels for 0%

profile of v1, /device:TPU:1, one launch (start us, length us, event | category | flops | bytes accessed | tf_op | source)
XLA Modules:
  0.0 327.2 jit_solution(9303991316539019739)
XLA Ops:
  6.5 0.7 fusion.54
  7.2 0.7 compare_and_fusion.4
  7.9 1.8 gather_fusion
  9.8 17.8 %all_to_all.5 = bf16[16,8,2048]{2,1,0:T(8,128)(2,1)S(1)} all-to-all(bf16[16,8,2048]{2,1,0:T(8,128)(2,1)S(1)} %broadcast_select_fusion.4), channel_id=1, replica_groups=mesh['group'=16,'member'=16] {'group'}, dimensions={0} | all-to-all | bytes 1048576 | tf_op jit(solution)/shard_map/all_to_all | solution.py:53
  27.6 2.5 pad_maximum_fusion.3
  30.1 2.1 fusion.63
  32.2 1.6 copy.82
  33.8 1.6 copy.89
  35.6 130.4 %all-gather.2.cloned.1.call-done = bf16[48,128,2048]{2,1,0:T(8,128)(2,1)} async-done(((bf16[48,8,2048]{2,1,0:T(8,128)(2,1)}), bf16[48,128,2048]{2,1,0:T(8,128)(2,1)}) %all-gather.2.cloned.1.call-update) | async-done | bytes 25165840 | tf_op jit(solution)/shard_map/all_gather | solution.py:55
  166.0 14.1 %split.8 = bf16[32,128,2048]{2,1,0:T(8,128)(2,1)} slice(bf16[48,128,2048]{2,1,0:T(8,128)(2,1)} %all-gather.2.cloned.1.call-done), slice={[0:32], [0:128], [0:2048]} | slice | bytes 33554432 | tf_op jit(solution)/shard_map/split | solution.py:54
  180.1 8.2 %gather_fusion.1 = bf16[5,128,2048]{2,1,0:T(8,128)(2,1)} fusion(bf16[32,128,2048]{2,1,0:T(8,128)(2,1)} %split.8, s32[1024]{0:T(1024)S(1)} %pad_clamp_fusion.3), kind=kCustom, calls=%fused_computation.clone | custom fusion | bytes 5242900 | tf_op jit(solution)/shard_map/jit(_take)/gather | solution.py:66
  188.3 8.1 %gather_fusion.3 = bf16[5,128,2048]{2,1,0:T(8,128)(2,1)} fusion(bf16[32,128,2048]{2,1,0:T(8,128)(2,1)} %split.8, s32[1024]{0:T(1024)S(1)} %pad_clamp_fusion.1), kind=kCustom, calls=%fused_computation.2.clone | custom fusion | bytes 5242900 | tf_op jit(solution)/shard_map/jit(_take)/gather | solution.py:66
  196.4 8.3 %split.9 = bf16[16,128,2048]{2,1,0:T(8,128)(2,1)} slice(bf16[48,128,2048]{2,1,0:T(8,128)(2,1)} %all-gather.2.cloned.1.call-done), slice={[32:48], [0:128], [0:2048]} | slice | bytes 16777216 | tf_op jit(solution)/shard_map/split | solution.py:54
  204.7 5.2 %gather_fusion.2 = bf16[3,128,2048]{2,1,0:T(8,128)(2,1)} fusion(bf16[16,128,2048]{2,1,0:T(8,128)(2,1)} %split.9, s32[1024]{0:T(1024)S(1)} %pad_clamp_fusion.2), kind=kCustom, calls=%fused_computation.1.clone | custom fusion | bytes 3145740 | tf_op jit(solution)/shard_map/jit(_take)/gather | solution.py:67
  209.9 5.2 %gather_fusion.4 = bf16[3,128,2048]{2,1,0:T(8,128)(2,1)} fusion(bf16[16,128,2048]{2,1,0:T(8,128)(2,1)} %split.9, s32[1024]{0:T(1024)S(1)} %pad_clamp_fusion), kind=kCustom, calls=%fused_computation.3.clone | custom fusion | bytes 3145740 | tf_op jit(solution)/shard_map/jit(_take)/gather | solution.py:67
  215.1 3.2 broadcast_select_fusion
  218.3 0.2 copy-done.2
  218.5 1.5 broadcast_select_fusion.2
  220.1 2.3 fusion.25
  222.3 3.9 %copy.34 = bf16[8,128,1024]{1,2,0:T(8,128)(2,1)} copy(bf16[8,128,1024]{2,1,0:T(8,128)(2,1)} %get-tuple-element.20) | data formatting | bytes 4194304 | tf_op jit(solution)/shard_map/slice | solution.py:16
  226.2 3.1 fusion.65
  229.3 2.3 copy.81
  231.6 2.3 copy.85
  233.9 3.9 %copy.32 = bf16[8,128,1024]{1,2,0:T(8,128)(2,1)} copy(bf16[8,128,1024]{2,1,0:T(8,128)(2,1)} %get-tuple-element.19) | data formatting | bytes 4194304 | tf_op jit(solution)/shard_map/slice | solution.py:19
  237.8 2.9 fusion.64
  240.7 6.3 %bitcast_reduce_fusion.3 = (f32[128,4,6]{0,2,1:T(8,128)S(1)}, f32[4,8,128,128,6]{3,2,4,1,0:T(8,128)}) fusion(pred[8]{0:T(512)(128)(4,1)S(1)} %get-tuple-element.51, bf16[128,8,6,128]{0,3,2,1:T(8,128)(2,1)S(1)} %bitcast.214, bf16[8,128,4,128]{3,1,0,2:T(8,128)(2,1)S(1)} %copy-done.3), kind=kOutput, calls=%fused_computation.15 | convolution fusion | flops 814740480 | bytes 14430720 | tf_op jit(solution)/shard_map/qgrd,pkgd->qgrpk/dot_general | solution.py:30
  247.0 7.4 %fusion.4 = (f32[128,4,6]{0,2,1:T(8,128)S(1)}, f32[128,4,6]{0,2,1:T(8,128)S(1)}, f32[4,8,128,128,6]{3,2,4,1,0:T(8,128)S(1)}) fusion(f32[4,8,128,128,6]{3,2,4,1,0:T(8,128)} %get-tuple-element.45, f32[128,4,6]{0,2,1:T(8,128)S(1)} %get-tuple-element.44, pred[8]{0:T(512)(128)(4,1)S(1)} %get-tuple-element.51, bf16[128,8,6,128]{0,3,2,1:T(8,128)(2,1)S(1)} %bitcast.215, ...), kind=kOutput, calls=%fused_computation.21 | convolution fusion | flops 827320320 | bytes 27042304 | tf_op jit(solution)/shard_map/qgrd,pkgd->qgrpk/dot_general | solution.py:30
  254.4 7.6 %fusion.29 = bf16[128,4,6,128]{0,3,2,1:T(8,128)(2,1)S(1)} fusion(f32[4,8,128,128,6]{3,2,4,1,0:T(8,128)} %get-tuple-element.45, f32[128,4,6]{0,2,1:T(8,128)S(1)} %get-tuple-element.44, pred[8]{0:T(512)(128)(4,1)S(1)} %get-tuple-element.51, bf16[8,128,4,128]{1,3,2,0:T(8,128)(2,1)S(1)} %get-tuple-element.25, f32[128,4,6]{0,2,1:T(8,128)S(1)} %get-tuple-element.6), kind=kOutput, calls=%fused_computation.55 | convolution fusion | flops 818675712 | bytes 14442504 | tf_op jit(solution)/shard_map/qgrpk,pkgd->qgrd/dot_general | solution.py:39
  262.0 2.5 fusion.6
  264.6 3.3 fusion.28
  267.9 1.3 pad_maximum_fusion.4
  269.1 2.6 copy.54
  271.7 3.4 %fusion.24 = (bf16[8,128,1024]{2,1,0:T(8,128)(2,1)}, bf16[8,128,1024]{2,1,0:T(8,128)(2,1)}) fusion(bf16[5,128,2048]{2,1,0:T(8,128)(2,1)S(1)} %get-tuple-element.47, bf16[3,128,2048]{2,1,0:T(8,128)(2,1)} %get-tuple-element.49), kind=kLoop, calls=%fused_computation.44 | loop fusion | flops 8388608 | bytes 8388608 | tf_op jit(solution)/shard_map/concatenate | solution.py:64
  275.1 3.0 copy.45
  278.2 1.5 fusion.67
  279.6 1.6 copy.88
  281.2 2.3 copy.92
  283.5 3.0 copy.43
  286.6 1.1 fusion.66
  287.7 0.7 copy-done.4
  288.4 6.3 %bitcast_reduce_fusion.1 = (f32[128,4,6]{0,2,1:T(8,128)S(1)}, f32[4,8,128,128,6]{3,2,4,1,0:T(8,128)}) fusion(pred[8]{0:T(512)(128)(4,1)S(1)} %get-tuple-element.52, bf16[128,8,6,128]{0,3,2,1:T(8,128)(2,1)S(1)} %bitcast.212, bf16[8,128,4,128]{3,1,0,2:T(8,128)(2,1)S(1)} %copy.88), kind=kOutput, calls=%fused_computation.9 | convolution fusion | flops 814740480 | bytes 14430720 | tf_op jit(solution)/shard_map/qgrd,pkgd->qgrpk/dot_general | solution.py:30
  294.7 7.2 %fusion.8 = (f32[128,4,6]{0,2,1:T(8,128)S(1)}, f32[128,4,6]{0,2,1:T(8,128)S(1)}, f32[4,8,128,128,6]{3,2,4,1,0:T(8,128)S(1)}) fusion(f32[4,8,128,128,6]{3,2,4,1,0:T(8,128)} %get-tuple-element.42, f32[128,4,6]{0,2,1:T(8,128)S(1)} %get-tuple-element.41, pred[8]{0:T(512)(128)(4,1)S(1)} %get-tuple-element.52, bf16[128,8,6,128]{0,3,2,1:T(8,128)(2,1)S(1)} %bitcast.213, ...), kind=kOutput, calls=%fused_computation.25 | convolution fusion | flops 827320320 | bytes 27042304 | tf_op jit(solution)/shard_map/qgrd,pkgd->qgrpk/dot_general | solution.py:30
  301.9 7.6 %fusion.27 = bf16[128,4,6,128]{0,3,2,1:T(8,128)(2,1)S(1)} fusion(f32[4,8,128,128,6]{3,2,4,1,0:T(8,128)} %get-tuple-element.42, f32[128,4,6]{0,2,1:T(8,128)S(1)} %get-tuple-element.41, pred[8]{0:T(512)(128)(4,1)S(1)} %get-tuple-element.52, bf16[8,128,4,128]{1,3,2,0:T(8,128)(2,1)S(1)} %get-tuple-element.29, f32[128,4,6]{0,2,1:T(8,128)S(1)} %get-tuple-element.9), kind=kOutput, calls=%fused_computation.51 | convolution fusion | flops 818675712 | bytes 14442504 | tf_op jit(solution)/shard_map/qgrpk,pkgd->qgrd/dot_general | solution.py:39
  309.5 2.5 fusion.10
  312.0 3.3 fusion.26
  315.3 0.1 pad_maximum_fusion.5
  315.4 1.6 copy.55
  317.0 3.4 %pad_maximum_fusion = bf16[256,6144]{1,0:T(8,128)(2,1)} fusion(bf16[128,6144]{1,0:T(8,128)(2,1)} %copy.55, bf16[128,6144]{1,0:T(8,128)(2,1)S(1)} %copy-done), kind=kLoop, calls=%fused_computation.41 | loop fusion | flops 6291456 | bytes 6291456 | tf_op jit(solution)/shard_map/concatenate | solution.py:74
  (35 shorter events, 0.3 us)
Async XLA Ops:
  6.5 159.5 %all-gather.2.cloned.1.call-start = ((), (), s32[]{:S(2)}) async-start(), calls=%async_computation.1 | async-start | bytes 26738688 | tf_op jit(solution)/shard_map/all_gather | solution.py:55
  32.2 3.2 copy-start.10
  32.2 3.2 copy-start.11
  215.1 3.2 copy-start.1
  215.1 3.4 %copy-start.2 = (bf16[3,128,2048]{2,1,0:T(8,128)(2,1)S(1)}, bf16[3,128,2048]{2,1,0:T(8,128)(2,1)}, u32[]{:S(2)}) copy-start(bf16[3,128,2048]{2,1,0:T(8,128)(2,1)} %gather_fusion.4) | copy-start | bytes 4718596
  237.8 2.9 copy-start.3
  237.8 2.9 copy-start.5
  240.7 6.3 %copy-start.7 = (bf16[8,128,4,128]{3,1,0,2:T(8,128)(2,1)S(1)}, bf16[8,128,4,128]{3,1,0,2:T(8,128)(2,1)}, u32[]{:S(2)}) copy-start(bf16[8,128,4,128]{3,1,0,2:T(8,128)(2,1)} %copy.85) | copy-start | bytes 3145732
  262.0 2.6 copy-start.9
  286.6 1.8 copy-start.4
  288.4 6.3 %copy-start.6 = (bf16[8,128,4,128]{3,1,0,2:T(8,128)(2,1)S(1)}, bf16[8,128,4,128]{3,1,0,2:T(8,128)(2,1)}, u32[]{:S(2)}) copy-start(bf16[8,128,4,128]{3,1,0,2:T(8,128)(2,1)} %copy.92) | copy-start | bytes 3145732
  309.5 2.5 copy-start.8
  315.3 1.8 copy-start
Sparse Core Ops, SparseCore 0:
  30.2 135.7 all-gather.1
